TPU v7x, 256 devices: a whole 4x4x8 slice. The times are simulated.
256 devices in a mesh: gx: 4 (over y), gy: 4 (over x), gz: 16 (over z, core).
Axes of the slice: x: 4, y: 4, z: 8, core: 2. Of those that a mesh axis runs over, the one named last changes fastest.
Arguments:
- rhs: float32 [4, 4, 16, 64, 1536], P('gx', 'gy', 'gz'), may hold values from -20 to 20
- dual_block: bfloat16 [4, 4, 16, 1536, 1536], P('gx', 'gy', 'gz'), may hold values from -1 to 4, as said below
- schur_block: bfloat16 [4, 4, 16, 1536, 1536], P('gx', 'gy', 'gz'), may hold values from -1 to 2, as said below
- dual_scale: float32 [4, 4, 16, 1536], P('gx', 'gy', 'gz'), may hold values from 0.5 to 1.5
- dof_order: int32 [4, 4, 16, 1536], P('gx', 'gy', 'gz'), may hold values from 0 to 1535, each once within a row
- modes: float32 [4, 4, 16, 1536, 24], P('gx', 'gy', 'gz'), may hold values from -0.21875 to 0.21875
- coarse_inverse: float32 [6144, 6144], P(('gx', 'gy', 'gz')), may hold values from -1 to 4, as said below
- step_scale: float32 [2], replicated, may hold values from 0.5 to 1
Outputs:
- multipliers: float32 [4, 4, 16, 64, 1536], P('gx', 'gy', 'gz')
- residual: float32 [4, 4, 16, 64, 1536], P('gx', 'gy', 'gz')
Inputs may be any that keep to these rules, and one draw needn't show every extreme that they name: For each subdomain, dof_order is a permutation of 0 to 1535. `dual_block`: Symmetric. `schur_block`: Symmetric. `coarse_inverse`: Symmetric.
All inputs are finite; a program needn't handle non-finite values.
Results may differ from a plain program's by a relative error of at most 0.0045.
Values sent between devices are 32-bit elements; how exact they have to be, the bound alone decides.
No kernel may reach another device: no remote copies, remote signals or barrier semaphores. Data moves between devices by JAX's collectives and lax.ppermute only.
A program may use at most 128 MiB of HBM per device.

v0:
```python
import jax
import jax.numpy as jnp
from jax import lax
from jax.sharding import PartitionSpec as P

ITERS = 2
HIGH = lax.Precision.HIGHEST


def extended(cells, sides, width):
    for axis, dim in sides:
        count = lax.axis_size(axis)
        ends = count - 1
        head = lax.slice_in_dim(cells, 0, width, axis=dim)
        tail = lax.slice_in_dim(cells, cells.shape[dim] - width, cells.shape[dim], axis=dim)
        cells = jnp.concatenate(
            [
                lax.ppermute(tail, axis, [(i, (i + 1) % count) for i in range(ends)]),
                cells,
                lax.ppermute(head, axis, [((i + 1) % count, i) for i in range(ends)]),
            ],
            axis=dim,
        )
    return cells


def reorder(matrix, order):
    rows = jnp.take(matrix, order, axis=0)
    return jnp.take(rows, order, axis=1)


def assemble(field):
    loads, width = field.shape
    faces = field.reshape(loads, 6, width // 6)
    ext_x = extended(jnp.stack([faces[:, 0], faces[:, 1]]), (("gx", 0),), 1)
    ext_y = extended(jnp.stack([faces[:, 2], faces[:, 3]]), (("gy", 0),), 1)
    ext_z = extended(jnp.stack([faces[:, 4], faces[:, 5]]), (("gz", 0),), 1)
    parts = [
        faces[:, 0] + ext_x[0],
        faces[:, 1] + ext_x[3],
        faces[:, 2] + ext_y[0],
        faces[:, 3] + ext_y[3],
        faces[:, 4] + ext_z[0],
        faces[:, 5] + ext_z[3],
    ]
    return jnp.stack(parts, axis=1).reshape(loads, width)


def project(field, basis, coarse_rows):
    weights = jnp.dot(field, basis, precision=HIGH)
    share = jnp.dot(
        lax.all_gather(weights, ("gx", "gy", "gz"), axis=1, tiled=True),
        coarse_rows.T,
        precision=HIGH,
    )
    correction = jnp.dot(share, basis.T, precision=HIGH)
    return field - assemble(correction)


def shards(rhs, dual_block, schur_block, dual_scale, dof_order, modes, coarse_inverse, step_scale):
    residual = rhs[0, 0, 0]
    order = dof_order[0, 0, 0]
    dual = reorder(dual_block[0, 0, 0], order)
    schur = reorder(schur_block[0, 0, 0], order)
    scale = dual_scale[0, 0, 0]
    basis = modes[0, 0, 0]

    def precondition(field):
        applied = jnp.dot(field.astype(jnp.bfloat16), schur, preferred_element_type=jnp.float32)
        return project(assemble(applied), basis, coarse_inverse)

    multipliers = jnp.zeros_like(residual)
    search = precondition(residual)
    for iteration in range(ITERS):
        image = scale * jnp.dot(
            (scale * search).astype(jnp.bfloat16), dual, preferred_element_type=jnp.float32
        )
        image = project(assemble(image), basis, coarse_inverse)
        later = iteration + 1 < ITERS
        along, energy = lax.psum(
            (jnp.sum(residual * image, axis=1), jnp.sum(image * image, axis=1)), ("gx", "gy", "gz")
        )
        alpha = step_scale[iteration] * along / (energy + 1e-06)
        multipliers = multipliers + alpha[:, None] * search
        residual = residual - alpha[:, None] * image
        if later:
            search = precondition(residual)
    return (multipliers[None, None, None], residual[None, None, None])


def solution(mesh):
    in_specs = (
        P("gx", "gy", "gz", None, None),
        P("gx", "gy", "gz", None, None),
        P("gx", "gy", "gz", None, None),
        P("gx", "gy", "gz", None),
        P("gx", "gy", "gz", None),
        P("gx", "gy", "gz", None, None),
        P(("gx", "gy", "gz"), None),
        P(),
    )
    out_specs = (P("gx", "gy", "gz", None, None), P("gx", "gy", "gz", None, None))
    return jax.shard_map(shards, mesh=mesh, in_specs=in_specs, out_specs=out_specs, check_vma=False)
```

profile of v0, /device:TPU:1, one launch (start us, length us, event | category | flops | bytes accessed | tf_op | source)
XLA Modules:
  0.0 909.4 jit_solution(9672217971376196631)
XLA Ops:
  8.0 13.3 %gather_fusion.2 = bf16[1536,1536]{1,0:T(8,128)(2,1)} fusion(bf16[1536,1536]{1,0:T(8,128)(2,1)} %bitcast.399, s32[2048]{0:T(1024)S(1)} %pad_clamp_fusion), kind=kCustom, calls=%fused_computation.2.clone | custom fusion | bytes 9443328 | tf_op jit(solution)/shard_map/jit(_take)/gather | solution.py:28
  21.4 13.3 %gather_fusion = bf16[1536,1536]{1,0:T(8,128)(2,1)} fusion(bf16[1536,1536]{1,0:T(8,128)(2,1)} %bitcast.400, s32[2048]{0:T(1024)S(1)} %pad_clamp_fusion), kind=kCustom, calls=%fused_computation.clone | custom fusion | bytes 9443328 | tf_op jit(solution)/shard_map/jit(_take)/gather | solution.py:28
  34.7 8.7 broadcast_select_fusion
  43.4 6.7 copy.72
  50.0 13.3 %gather_fusion.1 = bf16[1536,1536]{1,0:T(8,128)(2,1)} fusion(bf16[1536,1536]{0,1:T(8,128)(2,1)} %copy.72, s32[2048]{0:T(1024)S(1)} %pad_clamp_fusion), kind=kCustom, calls=%fused_computation.1.clone | custom fusion | bytes 9443328 | tf_op jit(solution)/shard_map/jit(_take)/gather | solution.py:29
  82.8 5.8 collective-permute-start.4
  98.3 111.7 %all-gather.5.cloned.1.call-done = f32[64,6144]{0,1:T(8,128)} async-done(((f32[64,24]{0,1:T(8,128)}), f32[64,6144]{0,1:T(8,128)}) %all-gather.5.cloned.1.call-update) | async-done | bytes 1572880 | tf_op jit(solution)/shard_map/all_gather | solution.py:52
  217.4 6.6 copy.82
  224.0 13.3 %gather_fusion.3 = bf16[1536,1536]{1,0:T(8,128)(2,1)} fusion(bf16[1536,1536]{0,1:T(8,128)(2,1)} %copy.82, s32[2048]{0:T(1024)S(1)} %pad_clamp_fusion), kind=kCustom, calls=%fused_computation.3.clone | custom fusion | bytes 9443328 | tf_op jit(solution)/shard_map/jit(_take)/gather | solution.py:29
  245.6 4.3 collective-permute-start.8
  255.6 4.2 collective-permute-start.12
  269.2 4.6 collective-permute-start.16
  282.4 109.9 %all-gather.7.cloned.1.call-done = f32[64,6144]{0,1:T(8,128)} async-done(((f32[64,24]{0,1:T(8,128)}), f32[64,6144]{0,1:T(8,128)}) %all-gather.7.cloned.1.call-update) | async-done | bytes 1572880 | tf_op jit(solution)/shard_map/all_gather | solution.py:52
  408.4 4.3 collective-permute-start.20
  415.7 79.7 %all-reduce.1 = (f32[64]{0:T(128)S(1)}, f32[64]{0:T(128)S(1)}) all-reduce(f32[64]{0:T(128)S(1)} %get-tuple-element.12, f32[64]{0:T(128)S(1)} %get-tuple-element.10), channel_id=1, replica_groups=mesh['gx'=4,'gy'=4,'gz'=16] {'gx','gy','gz'}, use_global_device_ids=true, to_apply=%region_3.6 | all-reduce | flops 128 | bytes 1024 | tf_op jit(solution)/shard_map/psum | solution.py:80
  509.4 4.3 collective-permute-start.26
  516.9 106.0 %all-gather.9.cloned.1.call-done = f32[64,6144]{0,1:T(8,128)} async-done(((f32[64,24]{0,1:T(8,128)}), f32[64,6144]{0,1:T(8,128)}) %all-gather.9.cloned.1.call-update) | async-done | bytes 1572880 | tf_op jit(solution)/shard_map/all_gather | solution.py:52
  638.4 4.3 collective-permute-start.32
  644.2 4.8 fusion.9
  653.7 4.2 collective-permute-start.36
  667.3 4.6 collective-permute-start.40
  680.5 110.0 %all-gather.11.cloned.1.call-done = f32[64,6144]{0,1:T(8,128)} async-done(((f32[64,24]{0,1:T(8,128)}), f32[64,6144]{0,1:T(8,128)}) %all-gather.11.cloned.1.call-update) | async-done | bytes 1572880 | tf_op jit(solution)/shard_map/all_gather | solution.py:52
  811.0 4.3 collective-permute-start.44
  821.3 78.8 %all-reduce = (f32[64]{0:T(128)S(1)}, f32[64]{0:T(128)S(1)}) all-reduce(f32[64]{0:T(128)S(1)} %get-tuple-element.8, f32[64]{0:T(128)S(1)} %fusion.17), channel_id=1, replica_groups=mesh['gx'=4,'gy'=4,'gz'=16] {'gx','gy','gz'}, use_global_device_ids=true, to_apply=%region_7.10 | all-reduce | flops 128 | bytes 1024 | tf_op jit(solution)/shard_map/psum | solution.py:80
  (236 shorter events, 173.3 us)
Async XLA Ops:
  7.2 202.9 %all-gather.5.cloned.1.call-start = ((), (), s32[]{:S(2)}) async-start(), calls=%async_computation | async-start | bytes 3158016 | tf_op jit(solution)/shard_map/all_gather | solution.py:52
  98.1 294.3 %all-gather.7.cloned.1.call-start = ((), (), s32[]{:S(2)}) async-start(), calls=%async_computation.1 | async-start | bytes 3158016 | tf_op jit(solution)/shard_map/all_gather | solution.py:52
  214.4 31.2 %collective-permute-start.6 = (f32[1,64,256]{2,1,0:T(8,128)S(1)}, f32[1,64,256]{2,1,0:T(8,128)S(1)}, u32[]{:S(2)}, u32[]{:S(2)}) collective-permute-start(f32[1,64,256]{2,1,0:T(8,128)S(1)} %get-tuple-element.61), channel_id=1, source_target_pairs={{0,64},{64,128},{128,192},{1,65},{65,129},{129,193},{2,66},{66,130... | collective-permute-start | bytes 196616 | tf_op jit(solution)/shard_map/ppermute | solution.py:18
  237.4 13.9 %collective-permute-start.11 = (f32[1,64,256]{2,1,0:T(8,128)S(1)}, f32[1,64,256]{2,1,0:T(8,128)S(1)}, u32[]{:S(2)}, u32[]{:S(2)}) collective-permute-start(f32[1,64,256]{2,1,0:T(8,128)S(1)} %get-tuple-element.56), channel_id=1, source_target_pairs={{1,0},{2,1},{3,2},{4,3},{5,4},{6,5},{7,6},{8,7},{9,8},{10,9},{11,1... | collective-permute-start | bytes 196616 | tf_op jit(solution)/shard_map/ppermute | solution.py:20
  239.9 10.0 %collective-permute-start.7 = (f32[1,64,256]{2,1,0:T(8,128)S(1)}, f32[1,64,256]{2,1,0:T(8,128)S(1)}, u32[]{:S(2)}, u32[]{:S(2)}) collective-permute-start(f32[1,64,256]{2,1,0:T(8,128)S(1)} %get-tuple-element.57), channel_id=1, source_target_pairs={{64,0},{128,64},{192,128},{65,1},{129,65},{193,129},{66,2},{130,66... | collective-permute-start | bytes 196616 | tf_op jit(solution)/shard_map/ppermute | solution.py:20
  241.2 10.1 %collective-permute-start.9 = (f32[1,64,256]{2,1,0:T(8,128)S(1)}, f32[1,64,256]{2,1,0:T(8,128)S(1)}, u32[]{:S(2)}, u32[]{:S(2)}) collective-permute-start(f32[1,64,256]{2,1,0:T(8,128)S(1)} %get-tuple-element.58), channel_id=1, source_target_pairs={{16,0},{32,16},{48,32},{17,1},{33,17},{49,33},{18,2},{34,18},{50,3... | collective-permute-start | bytes 196616 | tf_op jit(solution)/shard_map/ppermute | solution.py:20
  282.4 340.5 %all-gather.9.cloned.1.call-start = ((), (), s32[]{:S(2)}) async-start(), calls=%async_computation.2 | async-start | bytes 3158016 | tf_op jit(solution)/shard_map/all_gather | solution.py:52
  396.6 11.8 %collective-permute-start.18 = (f32[1,64,256]{2,1,0:T(8,128)S(1)}, f32[1,64,256]{2,1,0:T(8,128)S(1)}, u32[]{:S(2)}, u32[]{:S(2)}) collective-permute-start(f32[1,64,256]{2,1,0:T(8,128)S(1)} %get-tuple-element.55), channel_id=1, source_target_pairs={{0,64},{64,128},{128,192},{1,65},{65,129},{129,193},{2,66},{66,130... | collective-permute-start | bytes 196616 | tf_op jit(solution)/shard_map/ppermute | solution.py:18
  400.3 13.9 %collective-permute-start.23 = (f32[1,64,256]{2,1,0:T(8,128)S(1)}, f32[1,64,256]{2,1,0:T(8,128)S(1)}, u32[]{:S(2)}, u32[]{:S(2)}) collective-permute-start(f32[1,64,256]{2,1,0:T(8,128)S(1)} %get-tuple-element.50), channel_id=1, source_target_pairs={{1,0},{2,1},{3,2},{4,3},{5,4},{6,5},{7,6},{8,7},{9,8},{10,9},{11,1... | collective-permute-start | bytes 196616 | tf_op jit(solution)/shard_map/ppermute | solution.py:20
  402.7 10.0 %collective-permute-start.19 = (f32[1,64,256]{2,1,0:T(8,128)S(1)}, f32[1,64,256]{2,1,0:T(8,128)S(1)}, u32[]{:S(2)}, u32[]{:S(2)}) collective-permute-start(f32[1,64,256]{2,1,0:T(8,128)S(1)} %get-tuple-element.51), channel_id=1, source_target_pairs={{64,0},{128,64},{192,128},{65,1},{129,65},{193,129},{66,2},{130,66... | collective-permute-start | bytes 196616 | tf_op jit(solution)/shard_map/ppermute | solution.py:20
  404.0 10.1 %collective-permute-start.21 = (f32[1,64,256]{2,1,0:T(8,128)S(1)}, f32[1,64,256]{2,1,0:T(8,128)S(1)}, u32[]{:S(2)}, u32[]{:S(2)}) collective-permute-start(f32[1,64,256]{2,1,0:T(8,128)S(1)} %get-tuple-element.52), channel_id=1, source_target_pairs={{16,0},{32,16},{48,32},{17,1},{33,17},{49,33},{18,2},{34,18},{50,3... | collective-permute-start | bytes 196616 | tf_op jit(solution)/shard_map/ppermute | solution.py:20
  499.9 9.5 %collective-permute-start.24 = (f32[1,64,256]{2,1,0:T(8,128)S(1)}, f32[1,64,256]{2,1,0:T(8,128)S(1)}, u32[]{:S(2)}, u32[]{:S(2)}) collective-permute-start(f32[1,64,256]{2,1,0:T(8,128)S(1)} %get-tuple-element.49), channel_id=1, source_target_pairs={{0,64},{64,128},{128,192},{1,65},{65,129},{129,193},{2,66},{66,130... | collective-permute-start | bytes 196616 | tf_op jit(solution)/shard_map/ppermute | solution.py:18
  501.2 14.4 %collective-permute-start.29 = (f32[1,64,256]{2,1,0:T(8,128)S(1)}, f32[1,64,256]{2,1,0:T(8,128)S(1)}, u32[]{:S(2)}, u32[]{:S(2)}) collective-permute-start(f32[1,64,256]{2,1,0:T(8,128)S(1)} %get-tuple-element.44), channel_id=1, source_target_pairs={{1,0},{2,1},{3,2},{4,3},{5,4},{6,5},{7,6},{8,7},{9,8},{10,9},{11,1... | collective-permute-start | bytes 196616 | tf_op jit(solution)/shard_map/ppermute | solution.py:20
  504.1 9.6 %collective-permute-start.25 = (f32[1,64,256]{2,1,0:T(8,128)S(1)}, f32[1,64,256]{2,1,0:T(8,128)S(1)}, u32[]{:S(2)}, u32[]{:S(2)}) collective-permute-start(f32[1,64,256]{2,1,0:T(8,128)S(1)} %get-tuple-element.45), channel_id=1, source_target_pairs={{64,0},{128,64},{192,128},{65,1},{129,65},{193,129},{66,2},{130,66... | collective-permute-start | bytes 196616 | tf_op jit(solution)/shard_map/ppermute | solution.py:20
  505.4 10.2 %collective-permute-start.27 = (f32[1,64,256]{2,1,0:T(8,128)S(1)}, f32[1,64,256]{2,1,0:T(8,128)S(1)}, u32[]{:S(2)}, u32[]{:S(2)}) collective-permute-start(f32[1,64,256]{2,1,0:T(8,128)S(1)} %get-tuple-element.46), channel_id=1, source_target_pairs={{16,0},{32,16},{48,32},{17,1},{33,17},{49,33},{18,2},{34,18},{50,3... | collective-permute-start | bytes 196616 | tf_op jit(solution)/shard_map/ppermute | solution.py:20
  516.8 273.6 %all-gather.11.cloned.1.call-start = ((), (), s32[]{:S(2)}) async-start(), calls=%async_computation.3 | async-start | bytes 3158016 | tf_op jit(solution)/shard_map/all_gather | solution.py:52
  627.1 11.2 %collective-permute-start.30 = (f32[1,64,256]{2,1,0:T(8,128)S(1)}, f32[1,64,256]{2,1,0:T(8,128)S(1)}, u32[]{:S(2)}, u32[]{:S(2)}) collective-permute-start(f32[1,64,256]{2,1,0:T(8,128)S(1)} %get-tuple-element.43), channel_id=1, source_target_pairs={{0,64},{64,128},{128,192},{1,65},{65,129},{129,193},{2,66},{66,130... | collective-permute-start | bytes 196616 | tf_op jit(solution)/shard_map/ppermute | solution.py:18
  630.2 13.9 %collective-permute-start.35 = (f32[1,64,256]{2,1,0:T(8,128)S(1)}, f32[1,64,256]{2,1,0:T(8,128)S(1)}, u32[]{:S(2)}, u32[]{:S(2)}) collective-permute-start(f32[1,64,256]{2,1,0:T(8,128)S(1)} %get-tuple-element.38), channel_id=1, source_target_pairs={{1,0},{2,1},{3,2},{4,3},{5,4},{6,5},{7,6},{8,7},{9,8},{10,9},{11,1... | collective-permute-start | bytes 196616 | tf_op jit(solution)/shard_map/ppermute | solution.py:20
  632.6 10.0 %collective-permute-start.31 = (f32[1,64,256]{2,1,0:T(8,128)S(1)}, f32[1,64,256]{2,1,0:T(8,128)S(1)}, u32[]{:S(2)}, u32[]{:S(2)}) collective-permute-start(f32[1,64,256]{2,1,0:T(8,128)S(1)} %get-tuple-element.39), channel_id=1, source_target_pairs={{64,0},{128,64},{192,128},{65,1},{129,65},{193,129},{66,2},{130,66... | collective-permute-start | bytes 196616 | tf_op jit(solution)/shard_map/ppermute | solution.py:20
  633.9 10.1 %collective-permute-start.33 = (f32[1,64,256]{2,1,0:T(8,128)S(1)}, f32[1,64,256]{2,1,0:T(8,128)S(1)}, u32[]{:S(2)}, u32[]{:S(2)}) collective-permute-start(f32[1,64,256]{2,1,0:T(8,128)S(1)} %get-tuple-element.40), channel_id=1, source_target_pairs={{16,0},{32,16},{48,32},{17,1},{33,17},{49,33},{18,2},{34,18},{50,3... | collective-permute-start | bytes 196616 | tf_op jit(solution)/shard_map/ppermute | solution.py:20
  794.7 16.2 %collective-permute-start.42 = (f32[1,64,256]{2,1,0:T(8,128)S(1)}, f32[1,64,256]{2,1,0:T(8,128)}, u32[]{:S(2)}, u32[]{:S(2)}) collective-permute-start(f32[1,64,256]{2,1,0:T(8,128)S(1)} %get-tuple-element.37), channel_id=1, source_target_pairs={{0,64},{64,128},{128,192},{1,65},{65,129},{129,193},{2,66},{66,130... | collective-permute-start | bytes 196616 | tf_op jit(solution)/shard_map/ppermute | solution.py:18
  802.8 13.9 %collective-permute-start.47 = (f32[1,64,256]{2,1,0:T(8,128)S(1)}, f32[1,64,256]{2,1,0:T(8,128)S(1)}, u32[]{:S(2)}, u32[]{:S(2)}) collective-permute-start(f32[1,64,256]{2,1,0:T(8,128)S(1)} %get-tuple-element.32), channel_id=1, source_target_pairs={{1,0},{2,1},{3,2},{4,3},{5,4},{6,5},{7,6},{8,7},{9,8},{10,9},{11,1... | collective-permute-start | bytes 196616 | tf_op jit(solution)/shard_map/ppermute | solution.py:20
  805.3 10.9 %collective-permute-start.43 = (f32[1,64,256]{2,1,0:T(8,128)S(1)}, f32[1,64,256]{2,1,0:T(8,128)S(1)}, u32[]{:S(2)}, u32[]{:S(2)}) collective-permute-start(f32[1,64,256]{2,1,0:T(8,128)S(1)} %get-tuple-element.33), channel_id=1, source_target_pairs={{64,0},{128,64},{192,128},{65,1},{129,65},{193,129},{66,2},{130,66... | collective-permute-start | bytes 196616 | tf_op jit(solution)/shard_map/ppermute | solution.py:20
  806.6 10.1 %collective-permute-start.45 = (f32[1,64,256]{2,1,0:T(8,128)S(1)}, f32[1,64,256]{2,1,0:T(8,128)S(1)}, u32[]{:S(2)}, u32[]{:S(2)}) collective-permute-start(f32[1,64,256]{2,1,0:T(8,128)S(1)} %get-tuple-element.34), channel_id=1, source_target_pairs={{16,0},{32,16},{48,32},{17,1},{33,17},{49,33},{18,2},{34,18},{50,3... | collective-permute-start | bytes 196616 | tf_op jit(solution)/shard_map/ppermute | solution.py:20
  (41 other events, 910.5 us)
Sparse Core Ops, SparseCore 0:
  98.2 111.8 all-gather.4
  282.5 109.7 all-gather.6
  516.9 105.8 all-gather.8
  680.6 109.7 all-gather.10
where the time goes:
time: 912 us; the launch traced here: 909 us
  waiting for transfers between devices  468 us (51%)
  blocking collectives  159 us (17%)
  starting transfers between devices  129 us (14%)
  local copies, waits for them, and re-layouts  80.7 us (9%)
  matrix products  35.1 us (4%)
  other arithmetic  22.8 us (2%)
  between operations  15.2 us (2%)
    all_gather x4, waiting for transfers between devices, project(): lax.all_gather(weights, ('gx', 'gy', 'gz'), axis=1, tiled=True)  438 us
    psum x2, blocking collectives, shards(): lax.psum((jnp.sum(residual * image, axis=1), jnp.sum(image * image, axis=...  159 us
    ppermute x24, starting transfers between devices, extended(): lax.ppermute(tail, axis, [(i, (i + 1) % count) for i in range(ends)])  87.9 us
    ppermute x24, starting transfers between devices, extended(): lax.ppermute(head, axis, [((i + 1) % count, i) for i in range(ends)])  41.2 us
    gather x2, local copies, waits for them, and re-layouts, reorder(): return jnp.take(rows, order, axis=1)  26.7 us
    gather x2, local copies, waits for them, and re-layouts, reorder(): rows = jnp.take(matrix, order, axis=0)  26.7 us
  transfers between devices with their start and end apart: 52, of which 22 were waited for; matrix products, arithmetic and copies ran while one was open for 3% of the time, Pallas kernels for 0%

commit v1 on v0

--- a/solution.py
+++ b/solution.py
@@ -1,3 +1,4 @@
+import functools
 import jax
 import jax.numpy as jnp
 from jax import lax
@@ -5,6 +6,19 @@
 
 ITERS = 2
 HIGH = lax.Precision.HIGHEST
+
+
+def edit_the_set(z_in, group_axis, pos_dim):
+    kept_arr = jnp.concatenate(
+        jax.lax.all_to_all(
+            jnp.stack([z_in for _ in range(jax.lax.axis_size(group_axis))]), group_axis, 0, 0
+        ),
+        axis=pos_dim,
+    )
+    return kept_arr
+
+
+convert_columns = functools.partial(edit_the_set, group_axis=("gx", "gy", "gz"), pos_dim=1)
 
 
 def extended(cells, sides, width):
@@ -48,11 +62,7 @@
 
 def project(field, basis, coarse_rows):
     weights = jnp.dot(field, basis, precision=HIGH)
-    share = jnp.dot(
-        lax.all_gather(weights, ("gx", "gy", "gz"), axis=1, tiled=True),
-        coarse_rows.T,
-        precision=HIGH,
-    )
+    share = jnp.dot(convert_columns(weights), coarse_rows.T, precision=HIGH)
     correction = jnp.dot(share, basis.T, precision=HIGH)
     return field - assemble(correction)
 

time: 912 us -> 738 us (0.81)
  waiting for transfers between devices: 468 us -> 73.1 us
  blocking collectives: 159 us -> 319 us
  local copies, waits for them, and re-layouts: 80.7 us -> 110 us
  other arithmetic: 22.8 us -> 44 us
  starting transfers between devices: 129 us -> 146 us
  between operations: 15.2 us -> 2.56 us
    all_gather x4 -> x0, waiting for transfers between devices: 438 us -> none  [project(): lax.all_gather(weights, ('gx', 'gy', 'gz'), axis=1, tiled=True)]
    all_to_all x0 -> x3, blocking collectives: none -> 168 us  [edit_the_set(): jax.lax.all_to_all(jnp.stack([z_in for _ in range(jax.lax.axis_size(group...]
    all_to_all x0 -> x1, waiting for transfers between devices: none -> 43.6 us  [edit_the_set(): jax.lax.all_to_all(jnp.stack([z_in for _ in range(jax.lax.axis_size(group...]
    unnamed x35 -> x71, local copies, waits for them, and re-layouts: 3.03 us -> 37.4 us
    all_to_all x0 -> x4, other arithmetic: none -> 23.3 us  [edit_the_set(): jax.lax.all_to_all(jnp.stack([z_in for _ in range(jax.lax.axis_size(group...]
    all_to_all x0 -> x1, starting transfers between devices: none -> 18.1 us  [edit_the_set(): jax.lax.all_to_all(jnp.stack([z_in for _ in range(jax.lax.axis_size(group...]
  transfers between devices with their start and end apart: 52 -> 49, of which waited for: 22 -> 21; matrix products, arithmetic and copies ran while one was open for 3% -> 3% of each run, Pallas kernels for 0% -> 0%
where the time goes in v1:
time: 738 us; the launch traced here: 727 us
  blocking collectives  319 us (43%)
  starting transfers between devices  146 us (20%)
  local copies, waits for them, and re-layouts  110 us (15%)
  waiting for transfers between devices  73.1 us (10%)
  other arithmetic  44 us (6%)
  matrix products  32 us (4%)
    all_to_all x3, blocking collectives, edit_the_set(): jax.lax.all_to_all(jnp.stack([z_in for _ in range(jax.lax.axis_size(group...  168 us
    psum x2, blocking collectives, shards(): lax.psum((jnp.sum(residual * image, axis=1), jnp.sum(image * image, axis=...  151 us
    ppermute x24, starting transfers between devices, extended(): lax.ppermute(tail, axis, [(i, (i + 1) % count) for i in range(ends)])  90.2 us
    all_to_all x1, waiting for transfers between devices, edit_the_set(): jax.lax.all_to_all(jnp.stack([z_in for _ in range(jax.lax.axis_size(group...  43.6 us
    ppermute x24, starting transfers between devices, extended(): lax.ppermute(head, axis, [((i + 1) % count, i) for i in range(ends)])  37.5 us
    unnamed x71, local copies, waits for them, and re-layouts  37.4 us
    gather x2, local copies, waits for them, and re-layouts, reorder(): return jnp.take(rows, order, axis=1)  26.7 us
    gather x2, local copies, waits for them, and re-layouts, reorder(): rows = jnp.take(matrix, order, axis=0)  26.7 us
  transfers between devices with their start and end apart: 49, of which 21 were waited for; matrix products, arithmetic and copies ran while one was open for 3% of the time, Pallas kernels for 0%

profile of v1, /device:TPU:1, one launch (start us, length us, event | category | flops | bytes accessed | tf_op | source)
XLA Modules:
  0.0 727.0 jit_solution(18042276230818023962)
XLA Ops:
  1.5 13.4 %gather_fusion.2 = bf16[1536,1536]{1,0:T(8,128)(2,1)} fusion(bf16[1536,1536]{1,0:T(8,128)(2,1)} %bitcast.423, s32[2048]{0:T(1024)S(1)} %pad_clamp_fusion), kind=kCustom, calls=%fused_computation.2.clone | custom fusion | bytes 9443328 | tf_op jit(solution)/shard_map/jit(_take)/gather | solution.py:42
  14.8 13.3 %gather_fusion = bf16[1536,1536]{1,0:T(8,128)(2,1)} fusion(bf16[1536,1536]{1,0:T(8,128)(2,1)} %bitcast.424, s32[2048]{0:T(1024)S(1)} %pad_clamp_fusion), kind=kCustom, calls=%fused_computation.clone | custom fusion | bytes 9443328 | tf_op jit(solution)/shard_map/jit(_take)/gather | solution.py:42
  28.1 8.7 %broadcast_select_fusion = (bf16[1536,1536]{1,0:T(8,128)(2,1)}, bf16[1536,1536]{1,0:T(8,128)(2,1)}) fusion(bf16[1536,1536]{1,0:T(8,128)(2,1)} %gather_fusion.2, pred[1536]{0:T(1024)(128)(4,1)S(1)} %compare_and_fusion, bf16[1536,1536]{1,0:T(8,128)(2,1)} %gather_fusion), kind=kLoop, calls=%fused_computation.10 | loop fusion | flops 4718592 | bytes 18875904 | tf_op jit(solution)/shard_map/jit(_take)/select_n | solution.py:42
  36.8 6.6 copy.40
  43.5 13.4 %gather_fusion.1 = bf16[1536,1536]{1,0:T(8,128)(2,1)} fusion(bf16[1536,1536]{0,1:T(8,128)(2,1)} %copy.40, s32[2048]{0:T(1024)S(1)} %pad_clamp_fusion), kind=kCustom, calls=%fused_computation.1.clone | custom fusion | bytes 9443328 | tf_op jit(solution)/shard_map/jit(_take)/gather | solution.py:43
  76.3 5.8 collective-permute-start.4
  92.1 4.4 reshape.374
  96.6 18.1 %all-to-all-start = ((f32[256,1,1536]{2,1,0:T(1,128)}), f32[256,1,1536]{2,1,0:T(1,128)S(1)}, u32[]{:S(2)}, u32[]{:S(2)}) async-start(f32[256,1,1536]{2,1,0:T(1,128)} %reshape.374), calls=%async_computation | async-start | bytes 3145728 | tf_op jit(solution)/shard_map/all_to_all | solution.py:13
  114.8 43.6 %all-to-all-done = f32[256,1,1536]{2,1,0:T(1,128)S(1)} async-done(((f32[256,1,1536]{2,1,0:T(1,128)}), f32[256,1,1536]{2,1,0:T(1,128)S(1)}, u32[]{:S(2)}, u32[]{:S(2)}) %all-to-all-start) | async-done | bytes 1572896 | tf_op jit(solution)/shard_map/all_to_all | solution.py:13
  159.0 5.9 reduce.4
  174.8 6.7 copy.50
  181.5 13.4 %gather_fusion.3 = bf16[1536,1536]{1,0:T(8,128)(2,1)} fusion(bf16[1536,1536]{0,1:T(8,128)(2,1)} %copy.50, s32[2048]{0:T(1024)S(1)} %pad_clamp_fusion), kind=kCustom, calls=%fused_computation.3.clone | custom fusion | bytes 9443328 | tf_op jit(solution)/shard_map/jit(_take)/gather | solution.py:43
  203.0 4.7 collective-permute-start.8
  226.8 5.0 collective-permute-start.16
  245.5 56.5 %all_to_all.20 = f32[256,1,1536]{2,1,0:T(1,128)} all-to-all(f32[256,1,1536]{2,1,0:T(1,128)S(1)} %reshape.376), channel_id=1, replica_groups=mesh['gx'=4,'gy'=4,'gz'=16] {'gx','gy','gz'}, dimensions={0} | all-to-all | bytes 3145728 | tf_op jit(solution)/shard_map/all_to_all | solution.py:13
  302.0 5.8 reduce.5
  325.3 4.4 collective-permute-start.20
  332.4 75.9 %all-reduce.1 = (f32[64]{0:T(128)S(1)}, f32[64]{0:T(128)S(1)}) all-reduce(f32[64]{0:T(128)S(1)} %get-tuple-element.12, f32[64]{0:T(128)S(1)} %get-tuple-element.10), channel_id=1, replica_groups=mesh['gx'=4,'gy'=4,'gz'=16] {'gx','gy','gz'}, use_global_device_ids=true, to_apply=%region_3.6 | all-reduce | flops 128 | bytes 1024 | tf_op jit(solution)/shard_map/psum | solution.py:90
  434.8 54.8 %all_to_all.21 = f32[256,1,1536]{2,1,0:T(1,128)} all-to-all(f32[256,1,1536]{2,1,0:T(1,128)S(1)} %reshape.378), channel_id=1, replica_groups=mesh['gx'=4,'gy'=4,'gz'=16] {'gx','gy','gz'}, dimensions={0} | all-to-all | bytes 3145728 | tf_op jit(solution)/shard_map/all_to_all | solution.py:13
  489.6 5.8 reduce.6
  536.0 4.9 collective-permute-start.40
  555.2 56.8 %all_to_all.22 = f32[256,1,1536]{2,1,0:T(1,128)S(1)} all-to-all(f32[256,1,1536]{2,1,0:T(1,128)} %reshape.380), channel_id=1, replica_groups=mesh['gx'=4,'gy'=4,'gz'=16] {'gx','gy','gz'}, dimensions={0} | all-to-all | bytes 3145728 | tf_op jit(solution)/shard_map/all_to_all | solution.py:13
  612.0 5.9 reduce.7
  649.8 75.1 %all-reduce = (f32[64]{0:T(128)S(1)}, f32[64]{0:T(128)S(1)}) all-reduce(f32[64]{0:T(128)S(1)} %get-tuple-element.8, f32[64]{0:T(128)S(1)} %fusion.17), channel_id=1, replica_groups=mesh['gx'=4,'gy'=4,'gz'=16] {'gx','gy','gz'}, use_global_device_ids=true, to_apply=%region_7.10 | all-reduce | flops 128 | bytes 1024 | tf_op jit(solution)/shard_map/psum | solution.py:90
  (270 shorter events, 215.5 us)
Async XLA Ops:
  96.6 61.8 %all-to-all-start = ((f32[256,1,1536]{2,1,0:T(1,128)}), f32[256,1,1536]{2,1,0:T(1,128)S(1)}, u32[]{:S(2)}, u32[]{:S(2)}) async-start(f32[256,1,1536]{2,1,0:T(1,128)} %reshape.374), calls=%async_computation | async-start | bytes 3145728 | tf_op jit(solution)/shard_map/all_to_all | solution.py:13
  172.5 30.5 %collective-permute-start.6 = (f32[1,64,256]{2,1,0:T(8,128)S(1)}, f32[1,64,256]{2,1,0:T(8,128)S(1)}, u32[]{:S(2)}, u32[]{:S(2)}) collective-permute-start(f32[1,64,256]{2,1,0:T(8,128)S(1)} %get-tuple-element.61), channel_id=1, source_target_pairs={{0,64},{64,128},{128,192},{1,65},{65,129},{129,193},{2,66},{66,130... | collective-permute-start | bytes 196616 | tf_op jit(solution)/shard_map/ppermute | solution.py:32
  194.8 13.8 %collective-permute-start.11 = (f32[1,64,256]{2,1,0:T(8,128)S(1)}, f32[1,64,256]{2,1,0:T(8,128)S(1)}, u32[]{:S(2)}, u32[]{:S(2)}) collective-permute-start(f32[1,64,256]{2,1,0:T(8,128)S(1)} %get-tuple-element.56), channel_id=1, source_target_pairs={{1,0},{2,1},{3,2},{4,3},{5,4},{6,5},{7,6},{8,7},{9,8},{10,9},{11,1... | collective-permute-start | bytes 196616 | tf_op jit(solution)/shard_map/ppermute | solution.py:34
  196.8 11.0 %collective-permute-start.7 = (f32[1,64,256]{2,1,0:T(8,128)S(1)}, f32[1,64,256]{2,1,0:T(8,128)S(1)}, u32[]{:S(2)}, u32[]{:S(2)}) collective-permute-start(f32[1,64,256]{2,1,0:T(8,128)S(1)} %get-tuple-element.57), channel_id=1, source_target_pairs={{64,0},{128,64},{192,128},{65,1},{129,65},{193,129},{66,2},{130,66... | collective-permute-start | bytes 196616 | tf_op jit(solution)/shard_map/ppermute | solution.py:34
  198.1 10.6 %collective-permute-start.9 = (f32[1,64,256]{2,1,0:T(8,128)S(1)}, f32[1,64,256]{2,1,0:T(8,128)S(1)}, u32[]{:S(2)}, u32[]{:S(2)}) collective-permute-start(f32[1,64,256]{2,1,0:T(8,128)S(1)} %get-tuple-element.58), channel_id=1, source_target_pairs={{16,0},{32,16},{48,32},{17,1},{33,17},{49,33},{18,2},{34,18},{50,3... | collective-permute-start | bytes 196616 | tf_op jit(solution)/shard_map/ppermute | solution.py:34
  199.4 9.3 %collective-permute-start.10 = (f32[1,64,256]{2,1,0:T(8,128)S(1)}, f32[1,64,256]{2,1,0:T(8,128)S(1)}, u32[]{:S(2)}, u32[]{:S(2)}) collective-permute-start(f32[1,64,256]{2,1,0:T(8,128)S(1)} %get-tuple-element.59), channel_id=1, source_target_pairs={{0,1},{1,2},{2,3},{3,4},{4,5},{5,6},{6,7},{7,8},{8,9},{9,10},{10,1... | collective-permute-start | bytes 196616 | tf_op jit(solution)/shard_map/ppermute | solution.py:32
  314.3 11.0 %collective-permute-start.18 = (f32[1,64,256]{2,1,0:T(8,128)S(1)}, f32[1,64,256]{2,1,0:T(8,128)S(1)}, u32[]{:S(2)}, u32[]{:S(2)}) collective-permute-start(f32[1,64,256]{2,1,0:T(8,128)S(1)} %get-tuple-element.55), channel_id=1, source_target_pairs={{0,64},{64,128},{128,192},{1,65},{65,129},{129,193},{2,66},{66,130... | collective-permute-start | bytes 196616 | tf_op jit(solution)/shard_map/ppermute | solution.py:32
  317.1 13.8 %collective-permute-start.23 = (f32[1,64,256]{2,1,0:T(8,128)S(1)}, f32[1,64,256]{2,1,0:T(8,128)S(1)}, u32[]{:S(2)}, u32[]{:S(2)}) collective-permute-start(f32[1,64,256]{2,1,0:T(8,128)S(1)} %get-tuple-element.50), channel_id=1, source_target_pairs={{1,0},{2,1},{3,2},{4,3},{5,4},{6,5},{7,6},{8,7},{9,8},{10,9},{11,1... | collective-permute-start | bytes 196616 | tf_op jit(solution)/shard_map/ppermute | solution.py:34
  319.0 10.7 %collective-permute-start.19 = (f32[1,64,256]{2,1,0:T(8,128)S(1)}, f32[1,64,256]{2,1,0:T(8,128)S(1)}, u32[]{:S(2)}, u32[]{:S(2)}) collective-permute-start(f32[1,64,256]{2,1,0:T(8,128)S(1)} %get-tuple-element.51), channel_id=1, source_target_pairs={{64,0},{128,64},{192,128},{65,1},{129,65},{193,129},{66,2},{130,66... | collective-permute-start | bytes 196616 | tf_op jit(solution)/shard_map/ppermute | solution.py:34
  320.3 10.6 %collective-permute-start.21 = (f32[1,64,256]{2,1,0:T(8,128)S(1)}, f32[1,64,256]{2,1,0:T(8,128)S(1)}, u32[]{:S(2)}, u32[]{:S(2)}) collective-permute-start(f32[1,64,256]{2,1,0:T(8,128)S(1)} %get-tuple-element.52), channel_id=1, source_target_pairs={{16,0},{32,16},{48,32},{17,1},{33,17},{49,33},{18,2},{34,18},{50,3... | collective-permute-start | bytes 196616 | tf_op jit(solution)/shard_map/ppermute | solution.py:34
  321.6 9.3 %collective-permute-start.22 = (f32[1,64,256]{2,1,0:T(8,128)S(1)}, f32[1,64,256]{2,1,0:T(8,128)S(1)}, u32[]{:S(2)}, u32[]{:S(2)}) collective-permute-start(f32[1,64,256]{2,1,0:T(8,128)S(1)} %get-tuple-element.53), channel_id=1, source_target_pairs={{0,1},{1,2},{2,3},{3,4},{4,5},{5,6},{6,7},{7,8},{8,9},{9,10},{10,1... | collective-permute-start | bytes 196616 | tf_op jit(solution)/shard_map/ppermute | solution.py:32
  412.9 10.0 %collective-permute-start.24 = (f32[1,64,256]{2,1,0:T(8,128)S(1)}, f32[1,64,256]{2,1,0:T(8,128)S(1)}, u32[]{:S(2)}, u32[]{:S(2)}) collective-permute-start(f32[1,64,256]{2,1,0:T(8,128)S(1)} %get-tuple-element.49), channel_id=1, source_target_pairs={{0,64},{64,128},{128,192},{1,65},{65,129},{129,193},{2,66},{66,130... | collective-permute-start | bytes 196616 | tf_op jit(solution)/shard_map/ppermute | solution.py:32
  414.2 14.4 %collective-permute-start.29 = (f32[1,64,256]{2,1,0:T(8,128)S(1)}, f32[1,64,256]{2,1,0:T(8,128)S(1)}, u32[]{:S(2)}, u32[]{:S(2)}) collective-permute-start(f32[1,64,256]{2,1,0:T(8,128)S(1)} %get-tuple-element.44), channel_id=1, source_target_pairs={{1,0},{2,1},{3,2},{4,3},{5,4},{6,5},{7,6},{8,7},{9,8},{10,9},{11,1... | collective-permute-start | bytes 196616 | tf_op jit(solution)/shard_map/ppermute | solution.py:34
  417.1 10.1 %collective-permute-start.25 = (f32[1,64,256]{2,1,0:T(8,128)S(1)}, f32[1,64,256]{2,1,0:T(8,128)S(1)}, u32[]{:S(2)}, u32[]{:S(2)}) collective-permute-start(f32[1,64,256]{2,1,0:T(8,128)S(1)} %get-tuple-element.45), channel_id=1, source_target_pairs={{64,0},{128,64},{192,128},{65,1},{129,65},{193,129},{66,2},{130,66... | collective-permute-start | bytes 196616 | tf_op jit(solution)/shard_map/ppermute | solution.py:34
  418.4 10.2 %collective-permute-start.27 = (f32[1,64,256]{2,1,0:T(8,128)S(1)}, f32[1,64,256]{2,1,0:T(8,128)S(1)}, u32[]{:S(2)}, u32[]{:S(2)}) collective-permute-start(f32[1,64,256]{2,1,0:T(8,128)S(1)} %get-tuple-element.46), channel_id=1, source_target_pairs={{16,0},{32,16},{48,32},{17,1},{33,17},{49,33},{18,2},{34,18},{50,3... | collective-permute-start | bytes 196616 | tf_op jit(solution)/shard_map/ppermute | solution.py:34
  501.7 10.4 %collective-permute-start.30 = (f32[1,64,256]{2,1,0:T(8,128)S(1)}, f32[1,64,256]{2,1,0:T(8,128)S(1)}, u32[]{:S(2)}, u32[]{:S(2)}) collective-permute-start(f32[1,64,256]{2,1,0:T(8,128)S(1)} %get-tuple-element.43), channel_id=1, source_target_pairs={{0,64},{64,128},{128,192},{1,65},{65,129},{129,193},{2,66},{66,130... | collective-permute-start | bytes 196616 | tf_op jit(solution)/shard_map/ppermute | solution.py:32
  504.0 13.9 %collective-permute-start.35 = (f32[1,64,256]{2,1,0:T(8,128)S(1)}, f32[1,64,256]{2,1,0:T(8,128)S(1)}, u32[]{:S(2)}, u32[]{:S(2)}) collective-permute-start(f32[1,64,256]{2,1,0:T(8,128)S(1)} %get-tuple-element.38), channel_id=1, source_target_pairs={{1,0},{2,1},{3,2},{4,3},{5,4},{6,5},{7,6},{8,7},{9,8},{10,9},{11,1... | collective-permute-start | bytes 196616 | tf_op jit(solution)/shard_map/ppermute | solution.py:34
  505.9 10.6 %collective-permute-start.31 = (f32[1,64,256]{2,1,0:T(8,128)S(1)}, f32[1,64,256]{2,1,0:T(8,128)S(1)}, u32[]{:S(2)}, u32[]{:S(2)}) collective-permute-start(f32[1,64,256]{2,1,0:T(8,128)S(1)} %get-tuple-element.39), channel_id=1, source_target_pairs={{64,0},{128,64},{192,128},{65,1},{129,65},{193,129},{66,2},{130,66... | collective-permute-start | bytes 196616 | tf_op jit(solution)/shard_map/ppermute | solution.py:34
  507.2 10.6 %collective-permute-start.33 = (f32[1,64,256]{2,1,0:T(8,128)S(1)}, f32[1,64,256]{2,1,0:T(8,128)S(1)}, u32[]{:S(2)}, u32[]{:S(2)}) collective-permute-start(f32[1,64,256]{2,1,0:T(8,128)S(1)} %get-tuple-element.40), channel_id=1, source_target_pairs={{16,0},{32,16},{48,32},{17,1},{33,17},{49,33},{18,2},{34,18},{50,3... | collective-permute-start | bytes 196616 | tf_op jit(solution)/shard_map/ppermute | solution.py:34
  626.4 13.7 %collective-permute-start.42 = (f32[1,64,256]{2,1,0:T(8,128)}, f32[1,64,256]{2,1,0:T(8,128)}, u32[]{:S(2)}, u32[]{:S(2)}) collective-permute-start(f32[1,64,256]{2,1,0:T(8,128)} %get-tuple-element.37), channel_id=1, source_target_pairs={{0,64},{64,128},{128,192},{1,65},{65,129},{129,193},{2,66},{66,130... | collective-permute-start | bytes 196616 | tf_op jit(solution)/shard_map/ppermute | solution.py:32
  632.0 14.2 %collective-permute-start.47 = (f32[1,64,256]{2,1,0:T(8,128)S(1)}, f32[1,64,256]{2,1,0:T(8,128)S(1)}, u32[]{:S(2)}, u32[]{:S(2)}) collective-permute-start(f32[1,64,256]{2,1,0:T(8,128)S(1)} %get-tuple-element.32), channel_id=1, source_target_pairs={{1,0},{2,1},{3,2},{4,3},{5,4},{6,5},{7,6},{8,7},{9,8},{10,9},{11,1... | collective-permute-start | bytes 196616 | tf_op jit(solution)/shard_map/ppermute | solution.py:34
  633.9 11.4 %collective-permute-start.43 = (f32[1,64,256]{2,1,0:T(8,128)}, f32[1,64,256]{2,1,0:T(8,128)S(1)}, u32[]{:S(2)}, u32[]{:S(2)}) collective-permute-start(f32[1,64,256]{2,1,0:T(8,128)} %get-tuple-element.33), channel_id=1, source_target_pairs={{64,0},{128,64},{192,128},{65,1},{129,65},{193,129},{66,2},{130,66... | collective-permute-start | bytes 196616 | tf_op jit(solution)/shard_map/ppermute | solution.py:34
  635.2 10.9 %collective-permute-start.45 = (f32[1,64,256]{2,1,0:T(8,128)}, f32[1,64,256]{2,1,0:T(8,128)S(1)}, u32[]{:S(2)}, u32[]{:S(2)}) collective-permute-start(f32[1,64,256]{2,1,0:T(8,128)} %get-tuple-element.34), channel_id=1, source_target_pairs={{16,0},{32,16},{48,32},{17,1},{33,17},{49,33},{18,2},{34,18},{50,3... | collective-permute-start | bytes 196616 | tf_op jit(solution)/shard_map/ppermute | solution.py:34
  636.5 9.6 %collective-permute-start.46 = (f32[1,64,256]{2,1,0:T(8,128)}, f32[1,64,256]{2,1,0:T(8,128)S(1)}, u32[]{:S(2)}, u32[]{:S(2)}) collective-permute-start(f32[1,64,256]{2,1,0:T(8,128)} %get-tuple-element.35), channel_id=1, source_target_pairs={{0,1},{1,2},{2,3},{3,4},{4,5},{5,6},{6,7},{7,8},{8,9},{9,10},{10,1... | collective-permute-start | bytes 196616 | tf_op jit(solution)/shard_map/ppermute | solution.py:32
  (50 other events, 1019.6 us)
